TPU v7x, 32 devices: a whole 2x2x4 slice. The times are simulated.
32 devices in a mesh: groups: 2 (over y), site: 4 (over z), sample: 4 (over x, core).
Axes of the slice: x: 2, y: 2, z: 4, core: 2. Of those that a mesh axis runs over, the one named last changes fastest.
Arguments:
- site_tensor: bfloat16 [8, 2048, 2, 2048], P(('groups', 'site'), None, None, 'sample'), parts along dimension 0, may hold values from -0.25 to 0.25
- fronts_in: bfloat16 [3072, 2048], P(('groups', 'sample')), parts along dimension 0
- outcomes: int32 [8, 1536], P(('groups', 'site'), 'sample'), parts along dimension 0, may hold values from 0 to 1
- charges: int32 [10, 16], P('groups'), parts along dimension 0, may hold values from 0 to 3
Outputs:
- fronts_out: bfloat16 [8, 1536, 2048], P(('groups', 'site'), 'sample'), parts along dimension 0
- log_steps: float32 [8, 1536], P(('groups', 'site'), 'sample'), parts along dimension 0
There are 2 independent parts, one for each index of `groups`. A program takes and returns all parts, laid end to end along the dimension named above; each array names one. Nothing has to cross between parts.
All inputs are finite; a program needn't handle non-finite values.
Results may differ from a plain program's by a relative error of at most 0.012.
Values may be sent and summed in bfloat16 or wider, within the bound.
No kernel may reach another device: no remote copies, remote signals or barrier semaphores. Data moves between devices by JAX's collectives and lax.ppermute only.
A program may use at most 128 MiB of HBM per device.

v0:
```python
import jax
import jax.numpy as jnp
from jax import lax
from jax.sharding import PartitionSpec as P

BLOCK = 128
CHARGES = 4
epsilon = 1e-06


def shifted(array, axis, by):
    count = lax.axis_size(axis)
    pairs = [(i, i + by) for i in range(count) if 0 <= i + by < count]
    return lax.ppermute(array, axis, pairs)


def block_mask(left_charge, right_charge):
    phases = jnp.arange(2, dtype=jnp.int32)
    return (
        right_charge[None, None, :]
        == (left_charge[:, None, None] + phases[None, :, None]) % CHARGES
    )


def per_device(site_tensor, fronts_in, outcomes, charges):
    owner_idx = lax.axis_index("site")
    site_count = lax.axis_size("site")
    left_charge = lax.dynamic_index_in_dim(charges, owner_idx, 0, keepdims=False)
    right_charge = lax.dynamic_index_in_dim(charges, owner_idx + 1, 0, keepdims=False)
    micro_count = 8
    sections = micro_count + site_count - 1
    row_count = fronts_in.shape[0]
    gathered = lax.all_gather(site_tensor, "sample", axis=3, tiled=True)[0]
    bond_width = gathered.shape[0]
    blocks = bond_width // BLOCK
    allowed = block_mask(left_charge, right_charge).astype(gathered.dtype)
    masked = (
        gathered.reshape(blocks, BLOCK, 2, blocks, BLOCK) * allowed[:, None, :, :, None]
    ).reshape(bond_width, 2 * bond_width)
    micro_rows = row_count // micro_count
    picks_all = outcomes[0]

    def advance(front_rows, picks):
        products = jnp.dot(front_rows, masked, preferred_element_type=jnp.float32).reshape(
            micro_rows, 2, bond_width
        )
        chosen = jnp.where(picks[:, None] == 1, products[:, 1], products[:, 0])
        row_norm = jnp.sqrt(jnp.mean(chosen * chosen, axis=1) + epsilon)
        return ((chosen / row_norm[:, None]).astype(jnp.bfloat16), jnp.log(row_norm))

    def skipped(front_rows, picks):
        return (front_rows, jnp.zeros((micro_rows,), jnp.float32))

    def section(section_idx, loop_state):
        received, out_fronts, out_logs = loop_state
        micro_idx = section_idx - owner_idx
        active = (micro_idx >= 0) & (micro_idx < micro_count)
        row_start = jnp.clip(micro_idx, 0, micro_count - 1) * micro_rows
        first_rows = lax.dynamic_slice_in_dim(fronts_in, row_start, micro_rows, 0)
        incoming = jnp.where(owner_idx == 0, first_rows, received)
        picks = lax.dynamic_slice_in_dim(picks_all, row_start, micro_rows, 0)
        new_front, log_norm = lax.cond(active, advance, skipped, incoming, picks)
        old_front = lax.dynamic_slice_in_dim(out_fronts, row_start, micro_rows, 0)
        old_logs = lax.dynamic_slice_in_dim(out_logs, row_start, micro_rows, 0)
        out_fronts = lax.dynamic_update_slice_in_dim(
            out_fronts, jnp.where(active, new_front, old_front), row_start, 0
        )
        out_logs = lax.dynamic_update_slice_in_dim(
            out_logs, jnp.where(active, log_norm, old_logs), row_start, 0
        )
        passed = shifted(new_front, "site", 1)
        return (passed, out_fronts, out_logs)

    initial = (
        jnp.zeros((micro_rows, bond_width), jnp.bfloat16),
        jnp.zeros((row_count, bond_width), jnp.bfloat16),
        jnp.zeros((row_count,), jnp.float32),
    )
    final_state = lax.fori_loop(0, sections, section, initial)
    return (final_state[1][None], final_state[2][None])


def solution(mesh):
    in_specs = (
        P(("groups", "site"), None, None, "sample"),
        P(("groups", "sample"), None),
        P(("groups", "site"), "sample"),
        P("groups", None),
    )
    out_specs = (P(("groups", "site"), "sample", None), P(("groups", "site"), "sample"))
    return jax.shard_map(
        per_device, mesh=mesh, in_specs=in_specs, out_specs=out_specs, check_vma=False
    )
```

profile of v0, /device:TPU:24, one launch (start us, length us, event | category | flops | bytes accessed | tf_op | source)
XLA Modules:
  0.0 360.7 jit_solution(17284264981978438301)
XLA Ops:
  8.9 6.1 %mul.22 = bf16[16,128,2,16,128]{4,3,2,1,0:T(8,128)(2,1)} broadcast(bf16[16,2,16]{2,1,0:T(2,128)(2,1)S(1)} %compare_convert_fusion), dimensions={0,2,3} | broadcast | bytes 16778240 | tf_op jit(solution)/shard_map/mul | solution.py:38
  15.0 26.2 %mul.23 = bf16[2048,4096]{1,0:T(8,128)(2,1)} reshape(bf16[16,128,2,16,128]{4,3,2,1,0:T(8,128)(2,1)} %mul.22) | data formatting | bytes 33554432 | tf_op jit(solution)/shard_map/mul | solution.py:38
  41.1 77.5 %all-gather.2.cloned.1.call-done = bf16[1,2048,2,2048]{3,2,1,0:T(2,128)(2,1)} async-done(((bf16[1,2048,2,512]{3,2,1,0:T(2,128)(2,1)}), bf16[1,2048,2,2048]{3,2,1,0:T(2,128)(2,1)}) %all-gather.2.cloned.1.call-update) | async-done | bytes 16777232 | tf_op jit(solution)/shard_map/all_gather | solution.py:33
  118.7 13.1 %copy.10 = bf16[256,8,2,2048]{3,1,2,0:T(8,128)(2,1)S(1)} copy(bf16[256,8,2,2048]{3,2,1,0:T(2,128)(2,1)} %bitcast.29) | data formatting | bytes 33554432
  131.8 9.3 %mul.24 = bf16[2048,4096]{1,0:T(8,128)(2,1)} multiply(bf16[2048,4096]{1,0:T(8,128)(2,1)S(1)} %bitcast.28, bf16[2048,4096]{1,0:T(8,128)(2,1)S(1)} %copy-done) | non-fusion elementwise | flops 8388608 | bytes 50331648 | tf_op jit(solution)/shard_map/mul | solution.py:38
  141.3 211.4 %while.18 = (s32[]{:T(128)}, bf16[48,2048]{1,0:T(8,128)(2,1)S(1)}, bf16[384,2048]{1,0:T(8,128)(2,1)S(1)}, f32[384]{0:T(512)S(1)}, s32[]{:T(128)}, /*index=5*/pre...) while((s32[]{:T(128)}, bf16[48,2048]{1,0:T(8,128)(2,1)S(1)}, ...), condition=%wide.region_4.5_spmd, body=%wide.region_0.4_spmd.sunk | while | flops 806092992 | bytes 24644720 | solution.py:79
  141.4 1.0 dynamic-slice_select_fusion.2
  142.4 1.3 collective-permute-start
  143.9 7.4 %collective-permute-done = bf16[48,2048]{1,0:T(8,128)(2,1)S(1)} collective-permute-done((bf16[48,2048]{1,0:T(8,128)(2,1)S(1)}, bf16[48,2048]{1,0:T(8,128)(2,1)S(1)}, u32[]{:S(2)}, u32[]{:S(2)}) %collective-permute-start) | collective-permute-done | bytes 196640 | tf_op jit(solution)/shard_map/while/body/eval_jaxpr/ppermute | solution.py:14
  151.3 1.0 dynamic-slice_select_fusion.2
  152.4 1.3 collective-permute-start
  153.9 6.6 %collective-permute-done = bf16[48,2048]{1,0:T(8,128)(2,1)S(1)} collective-permute-done((bf16[48,2048]{1,0:T(8,128)(2,1)S(1)}, bf16[48,2048]{1,0:T(8,128)(2,1)S(1)}, u32[]{:S(2)}, u32[]{:S(2)}) %collective-permute-start) | collective-permute-done | bytes 196640 | tf_op jit(solution)/shard_map/while/body/eval_jaxpr/ppermute | solution.py:14
  160.4 1.0 dynamic-slice_select_fusion.2
  161.5 1.3 collective-permute-start
  163.0 34.7 %collective-permute-done = bf16[48,2048]{1,0:T(8,128)(2,1)S(1)} collective-permute-done((bf16[48,2048]{1,0:T(8,128)(2,1)S(1)}, bf16[48,2048]{1,0:T(8,128)(2,1)S(1)}, u32[]{:S(2)}, u32[]{:S(2)}) %collective-permute-start) | collective-permute-done | bytes 196640 | tf_op jit(solution)/shard_map/while/body/eval_jaxpr/ppermute | solution.py:14
  198.7 10.8 %conditional.2 = (bf16[48,2048]{1,0:T(8,128)(2,1)S(1)}, f32[48]{0:T(128)S(1)}) conditional(s32[]{:T(128)} %convert_element_type.22, bf16[48,2048]{1,0:T(8,128)(2,1)S(1)} %dynamic-slice_select_fusion.2, (s32[384]{0:T(512)S(1)}, s32[]{:T(128)}, bf16[48,2048]{1,0:T(8,128)(2,1)S(1)}, bf16[2048,4096]{1,0:T(8,128)(2,1)}) %tuple.53), branch_computations={%region_1.1_spmd, %region_2.3_spmd} | conditional | flops 805896320 | bytes 22676772 | solution.py:62
  198.7 8.8 %fusion.8 = f32[48,4096]{1,0:T(8,128)S(1)} fusion(bf16[48,2048]{1,0:T(8,128)(2,1)S(1)} %get-tuple-element.177, bf16[2048,4096]{1,0:T(8,128)(2,1)} %get-tuple-element.178), kind=kOutput, calls=%fused_computation.24 | convolution fusion | flops 805306368 | bytes 17760256 | tf_op jit(solution)/shard_map/while/body/eval_jaxpr/cond/branch_1_fun/dot_general | solution.py:44
  209.5 1.3 collective-permute-start
  211.1 6.0 %collective-permute-done = bf16[48,2048]{1,0:T(8,128)(2,1)S(1)} collective-permute-done((bf16[48,2048]{1,0:T(8,128)(2,1)S(1)}, bf16[48,2048]{1,0:T(8,128)(2,1)S(1)}, u32[]{:S(2)}, u32[]{:S(2)}) %collective-permute-start) | collective-permute-done | bytes 196640 | tf_op jit(solution)/shard_map/while/body/eval_jaxpr/ppermute | solution.py:14
  218.1 10.8 %conditional.2 = (bf16[48,2048]{1,0:T(8,128)(2,1)S(1)}, f32[48]{0:T(128)S(1)}) conditional(s32[]{:T(128)} %convert_element_type.22, bf16[48,2048]{1,0:T(8,128)(2,1)S(1)} %dynamic-slice_select_fusion.2, (s32[384]{0:T(512)S(1)}, s32[]{:T(128)}, bf16[48,2048]{1,0:T(8,128)(2,1)S(1)}, bf16[2048,4096]{1,0:T(8,128)(2,1)}) %tuple.53), branch_computations={%region_1.1_spmd, %region_2.3_spmd} | conditional | flops 805896320 | bytes 22676772 | solution.py:62
  218.1 8.8 %fusion.8 = f32[48,4096]{1,0:T(8,128)S(1)} fusion(bf16[48,2048]{1,0:T(8,128)(2,1)S(1)} %get-tuple-element.177, bf16[2048,4096]{1,0:T(8,128)(2,1)} %get-tuple-element.178), kind=kOutput, calls=%fused_computation.24 | convolution fusion | flops 805306368 | bytes 17760256 | tf_op jit(solution)/shard_map/while/body/eval_jaxpr/cond/branch_1_fun/dot_general | solution.py:44
  228.9 1.3 collective-permute-start
  230.4 6.0 %collective-permute-done = bf16[48,2048]{1,0:T(8,128)(2,1)S(1)} collective-permute-done((bf16[48,2048]{1,0:T(8,128)(2,1)S(1)}, bf16[48,2048]{1,0:T(8,128)(2,1)S(1)}, u32[]{:S(2)}, u32[]{:S(2)}) %collective-permute-start) | collective-permute-done | bytes 196640 | tf_op jit(solution)/shard_map/while/body/eval_jaxpr/ppermute | solution.py:14
  237.5 10.8 %conditional.2 = (bf16[48,2048]{1,0:T(8,128)(2,1)S(1)}, f32[48]{0:T(128)S(1)}) conditional(s32[]{:T(128)} %convert_element_type.22, bf16[48,2048]{1,0:T(8,128)(2,1)S(1)} %dynamic-slice_select_fusion.2, (s32[384]{0:T(512)S(1)}, s32[]{:T(128)}, bf16[48,2048]{1,0:T(8,128)(2,1)S(1)}, bf16[2048,4096]{1,0:T(8,128)(2,1)}) %tuple.53), branch_computations={%region_1.1_spmd, %region_2.3_spmd} | conditional | flops 805896320 | bytes 22676772 | solution.py:62
  237.5 8.8 %fusion.8 = f32[48,4096]{1,0:T(8,128)S(1)} fusion(bf16[48,2048]{1,0:T(8,128)(2,1)S(1)} %get-tuple-element.177, bf16[2048,4096]{1,0:T(8,128)(2,1)} %get-tuple-element.178), kind=kOutput, calls=%fused_computation.24 | convolution fusion | flops 805306368 | bytes 17760256 | tf_op jit(solution)/shard_map/while/body/eval_jaxpr/cond/branch_1_fun/dot_general | solution.py:44
  248.3 1.3 collective-permute-start
  249.8 6.0 %collective-permute-done = bf16[48,2048]{1,0:T(8,128)(2,1)S(1)} collective-permute-done((bf16[48,2048]{1,0:T(8,128)(2,1)S(1)}, bf16[48,2048]{1,0:T(8,128)(2,1)S(1)}, u32[]{:S(2)}, u32[]{:S(2)}) %collective-permute-start) | collective-permute-done | bytes 196640 | tf_op jit(solution)/shard_map/while/body/eval_jaxpr/ppermute | solution.py:14
  256.8 10.8 %conditional.2 = (bf16[48,2048]{1,0:T(8,128)(2,1)S(1)}, f32[48]{0:T(128)S(1)}) conditional(s32[]{:T(128)} %convert_element_type.22, bf16[48,2048]{1,0:T(8,128)(2,1)S(1)} %dynamic-slice_select_fusion.2, (s32[384]{0:T(512)S(1)}, s32[]{:T(128)}, bf16[48,2048]{1,0:T(8,128)(2,1)S(1)}, bf16[2048,4096]{1,0:T(8,128)(2,1)}) %tuple.53), branch_computations={%region_1.1_spmd, %region_2.3_spmd} | conditional | flops 805896320 | bytes 22676772 | solution.py:62
  256.8 8.8 %fusion.8 = f32[48,4096]{1,0:T(8,128)S(1)} fusion(bf16[48,2048]{1,0:T(8,128)(2,1)S(1)} %get-tuple-element.177, bf16[2048,4096]{1,0:T(8,128)(2,1)} %get-tuple-element.178), kind=kOutput, calls=%fused_computation.24 | convolution fusion | flops 805306368 | bytes 17760256 | tf_op jit(solution)/shard_map/while/body/eval_jaxpr/cond/branch_1_fun/dot_general | solution.py:44
  267.7 1.3 collective-permute-start
  269.2 6.0 %collective-permute-done = bf16[48,2048]{1,0:T(8,128)(2,1)S(1)} collective-permute-done((bf16[48,2048]{1,0:T(8,128)(2,1)S(1)}, bf16[48,2048]{1,0:T(8,128)(2,1)S(1)}, u32[]{:S(2)}, u32[]{:S(2)}) %collective-permute-start) | collective-permute-done | bytes 196640 | tf_op jit(solution)/shard_map/while/body/eval_jaxpr/ppermute | solution.py:14
  276.2 10.8 %conditional.2 = (bf16[48,2048]{1,0:T(8,128)(2,1)S(1)}, f32[48]{0:T(128)S(1)}) conditional(s32[]{:T(128)} %convert_element_type.22, bf16[48,2048]{1,0:T(8,128)(2,1)S(1)} %dynamic-slice_select_fusion.2, (s32[384]{0:T(512)S(1)}, s32[]{:T(128)}, bf16[48,2048]{1,0:T(8,128)(2,1)S(1)}, bf16[2048,4096]{1,0:T(8,128)(2,1)}) %tuple.53), branch_computations={%region_1.1_spmd, %region_2.3_spmd} | conditional | flops 805896320 | bytes 22676772 | solution.py:62
  276.2 8.8 %fusion.8 = f32[48,4096]{1,0:T(8,128)S(1)} fusion(bf16[48,2048]{1,0:T(8,128)(2,1)S(1)} %get-tuple-element.177, bf16[2048,4096]{1,0:T(8,128)(2,1)} %get-tuple-element.178), kind=kOutput, calls=%fused_computation.24 | convolution fusion | flops 805306368 | bytes 17760256 | tf_op jit(solution)/shard_map/while/body/eval_jaxpr/cond/branch_1_fun/dot_general | solution.py:44
  287.0 1.3 collective-permute-start
  288.6 6.0 %collective-permute-done = bf16[48,2048]{1,0:T(8,128)(2,1)S(1)} collective-permute-done((bf16[48,2048]{1,0:T(8,128)(2,1)S(1)}, bf16[48,2048]{1,0:T(8,128)(2,1)S(1)}, u32[]{:S(2)}, u32[]{:S(2)}) %collective-permute-start) | collective-permute-done | bytes 196640 | tf_op jit(solution)/shard_map/while/body/eval_jaxpr/ppermute | solution.py:14
  295.6 10.8 %conditional.2 = (bf16[48,2048]{1,0:T(8,128)(2,1)S(1)}, f32[48]{0:T(128)S(1)}) conditional(s32[]{:T(128)} %convert_element_type.22, bf16[48,2048]{1,0:T(8,128)(2,1)S(1)} %dynamic-slice_select_fusion.2, (s32[384]{0:T(512)S(1)}, s32[]{:T(128)}, bf16[48,2048]{1,0:T(8,128)(2,1)S(1)}, bf16[2048,4096]{1,0:T(8,128)(2,1)}) %tuple.53), branch_computations={%region_1.1_spmd, %region_2.3_spmd} | conditional | flops 805896320 | bytes 22676772 | solution.py:62
  295.6 8.8 %fusion.8 = f32[48,4096]{1,0:T(8,128)S(1)} fusion(bf16[48,2048]{1,0:T(8,128)(2,1)S(1)} %get-tuple-element.177, bf16[2048,4096]{1,0:T(8,128)(2,1)} %get-tuple-element.178), kind=kOutput, calls=%fused_computation.24 | convolution fusion | flops 805306368 | bytes 17760256 | tf_op jit(solution)/shard_map/while/body/eval_jaxpr/cond/branch_1_fun/dot_general | solution.py:44
  306.4 1.3 collective-permute-start
  307.9 6.0 %collective-permute-done = bf16[48,2048]{1,0:T(8,128)(2,1)S(1)} collective-permute-done((bf16[48,2048]{1,0:T(8,128)(2,1)S(1)}, bf16[48,2048]{1,0:T(8,128)(2,1)S(1)}, u32[]{:S(2)}, u32[]{:S(2)}) %collective-permute-start) | collective-permute-done | bytes 196640 | tf_op jit(solution)/shard_map/while/body/eval_jaxpr/ppermute | solution.py:14
  315.0 10.8 %conditional.2 = (bf16[48,2048]{1,0:T(8,128)(2,1)S(1)}, f32[48]{0:T(128)S(1)}) conditional(s32[]{:T(128)} %convert_element_type.22, bf16[48,2048]{1,0:T(8,128)(2,1)S(1)} %dynamic-slice_select_fusion.2, (s32[384]{0:T(512)S(1)}, s32[]{:T(128)}, bf16[48,2048]{1,0:T(8,128)(2,1)S(1)}, bf16[2048,4096]{1,0:T(8,128)(2,1)}) %tuple.53), branch_computations={%region_1.1_spmd, %region_2.3_spmd} | conditional | flops 805896320 | bytes 22676772 | solution.py:62
  315.0 8.8 %fusion.8 = f32[48,4096]{1,0:T(8,128)S(1)} fusion(bf16[48,2048]{1,0:T(8,128)(2,1)S(1)} %get-tuple-element.177, bf16[2048,4096]{1,0:T(8,128)(2,1)} %get-tuple-element.178), kind=kOutput, calls=%fused_computation.24 | convolution fusion | flops 805306368 | bytes 17760256 | tf_op jit(solution)/shard_map/while/body/eval_jaxpr/cond/branch_1_fun/dot_general | solution.py:44
  325.8 1.3 collective-permute-start
  327.3 6.0 %collective-permute-done = bf16[48,2048]{1,0:T(8,128)(2,1)S(1)} collective-permute-done((bf16[48,2048]{1,0:T(8,128)(2,1)S(1)}, bf16[48,2048]{1,0:T(8,128)(2,1)S(1)}, u32[]{:S(2)}, u32[]{:S(2)}) %collective-permute-start) | collective-permute-done | bytes 196640 | tf_op jit(solution)/shard_map/while/body/eval_jaxpr/ppermute | solution.py:14
  333.3 1.0 dynamic-slice_select_fusion.2
  334.3 10.8 %conditional.2 = (bf16[48,2048]{1,0:T(8,128)(2,1)S(1)}, f32[48]{0:T(128)S(1)}) conditional(s32[]{:T(128)} %convert_element_type.22, bf16[48,2048]{1,0:T(8,128)(2,1)S(1)} %dynamic-slice_select_fusion.2, (s32[384]{0:T(512)S(1)}, s32[]{:T(128)}, bf16[48,2048]{1,0:T(8,128)(2,1)S(1)}, bf16[2048,4096]{1,0:T(8,128)(2,1)}) %tuple.53), branch_computations={%region_1.1_spmd, %region_2.3_spmd} | conditional | flops 805896320 | bytes 22676772 | solution.py:62
  334.3 8.8 %fusion.8 = f32[48,4096]{1,0:T(8,128)S(1)} fusion(bf16[48,2048]{1,0:T(8,128)(2,1)S(1)} %get-tuple-element.177, bf16[2048,4096]{1,0:T(8,128)(2,1)} %get-tuple-element.178), kind=kOutput, calls=%fused_computation.24 | convolution fusion | flops 805306368 | bytes 17760256 | tf_op jit(solution)/shard_map/while/body/eval_jaxpr/cond/branch_1_fun/dot_general | solution.py:44
  345.2 1.3 collective-permute-start
  346.7 6.0 %collective-permute-done = bf16[48,2048]{1,0:T(8,128)(2,1)S(1)} collective-permute-done((bf16[48,2048]{1,0:T(8,128)(2,1)S(1)}, bf16[48,2048]{1,0:T(8,128)(2,1)S(1)}, u32[]{:S(2)}, u32[]{:S(2)}) %collective-permute-start) | collective-permute-done | bytes 196640 | tf_op jit(solution)/shard_map/while/body/eval_jaxpr/ppermute | solution.py:14
  (99 shorter events, 28.4 us)
Async XLA Ops:
  7.2 111.5 %all-gather.2.cloned.1.call-start = ((), (), s32[]{:S(2)}) async-start(), calls=%async_computation | async-start | bytes 20971520 | tf_op jit(solution)/shard_map/all_gather | solution.py:33
  14.9 26.2 %copy-start.2 = (s32[1,384]{1,0:T(1,128)S(1)}, s32[1,384]{1,0:T(1,128)}, u32[]{:S(2)}) copy-start(s32[1,384]{1,0:T(1,128)} %param.10) | copy-start | bytes 4612
  118.7 13.2 %copy-start = (bf16[2048,4096]{1,0:T(8,128)(2,1)S(1)}, bf16[2048,4096]{1,0:T(8,128)(2,1)}, u32[]{:S(2)}) copy-start(bf16[2048,4096]{1,0:T(8,128)(2,1)} %mul.23) | copy-start | bytes 50331652
  142.4 9.0 %collective-permute-start = (bf16[48,2048]{1,0:T(8,128)(2,1)S(1)}, bf16[48,2048]{1,0:T(8,128)(2,1)S(1)}, u32[]{:S(2)}, u32[]{:S(2)}) collective-permute-start(bf16[48,2048]{1,0:T(8,128)(2,1)S(1)} %get-tuple-element.278), channel_id=1, source_target_pairs={{0,4},{4,8},{8,12},{1,5},{5,9},{9,13},{2,6},{6,10},{10,14},{3,7},{... | collective-permute-start | bytes 589832 | tf_op jit(solution)/shard_map/while/body/eval_jaxpr/ppermute | solution.py:14
  152.4 8.1 %collective-permute-start = (bf16[48,2048]{1,0:T(8,128)(2,1)S(1)}, bf16[48,2048]{1,0:T(8,128)(2,1)S(1)}, u32[]{:S(2)}, u32[]{:S(2)}) collective-permute-start(bf16[48,2048]{1,0:T(8,128)(2,1)S(1)} %get-tuple-element.278), channel_id=1, source_target_pairs={{0,4},{4,8},{8,12},{1,5},{5,9},{9,13},{2,6},{6,10},{10,14},{3,7},{... | collective-permute-start | bytes 589832 | tf_op jit(solution)/shard_map/while/body/eval_jaxpr/ppermute | solution.py:14
  161.5 36.3 %collective-permute-start = (bf16[48,2048]{1,0:T(8,128)(2,1)S(1)}, bf16[48,2048]{1,0:T(8,128)(2,1)S(1)}, u32[]{:S(2)}, u32[]{:S(2)}) collective-permute-start(bf16[48,2048]{1,0:T(8,128)(2,1)S(1)} %get-tuple-element.278), channel_id=1, source_target_pairs={{0,4},{4,8},{8,12},{1,5},{5,9},{9,13},{2,6},{6,10},{10,14},{3,7},{... | collective-permute-start | bytes 589832 | tf_op jit(solution)/shard_map/while/body/eval_jaxpr/ppermute | solution.py:14
  209.5 7.6 %collective-permute-start = (bf16[48,2048]{1,0:T(8,128)(2,1)S(1)}, bf16[48,2048]{1,0:T(8,128)(2,1)S(1)}, u32[]{:S(2)}, u32[]{:S(2)}) collective-permute-start(bf16[48,2048]{1,0:T(8,128)(2,1)S(1)} %get-tuple-element.278), channel_id=1, source_target_pairs={{0,4},{4,8},{8,12},{1,5},{5,9},{9,13},{2,6},{6,10},{10,14},{3,7},{... | collective-permute-start | bytes 589832 | tf_op jit(solution)/shard_map/while/body/eval_jaxpr/ppermute | solution.py:14
  228.9 7.6 %collective-permute-start = (bf16[48,2048]{1,0:T(8,128)(2,1)S(1)}, bf16[48,2048]{1,0:T(8,128)(2,1)S(1)}, u32[]{:S(2)}, u32[]{:S(2)}) collective-permute-start(bf16[48,2048]{1,0:T(8,128)(2,1)S(1)} %get-tuple-element.278), channel_id=1, source_target_pairs={{0,4},{4,8},{8,12},{1,5},{5,9},{9,13},{2,6},{6,10},{10,14},{3,7},{... | collective-permute-start | bytes 589832 | tf_op jit(solution)/shard_map/while/body/eval_jaxpr/ppermute | solution.py:14
  248.3 7.6 %collective-permute-start = (bf16[48,2048]{1,0:T(8,128)(2,1)S(1)}, bf16[48,2048]{1,0:T(8,128)(2,1)S(1)}, u32[]{:S(2)}, u32[]{:S(2)}) collective-permute-start(bf16[48,2048]{1,0:T(8,128)(2,1)S(1)} %get-tuple-element.278), channel_id=1, source_target_pairs={{0,4},{4,8},{8,12},{1,5},{5,9},{9,13},{2,6},{6,10},{10,14},{3,7},{... | collective-permute-start | bytes 589832 | tf_op jit(solution)/shard_map/while/body/eval_jaxpr/ppermute | solution.py:14
  267.7 7.6 %collective-permute-start = (bf16[48,2048]{1,0:T(8,128)(2,1)S(1)}, bf16[48,2048]{1,0:T(8,128)(2,1)S(1)}, u32[]{:S(2)}, u32[]{:S(2)}) collective-permute-start(bf16[48,2048]{1,0:T(8,128)(2,1)S(1)} %get-tuple-element.278), channel_id=1, source_target_pairs={{0,4},{4,8},{8,12},{1,5},{5,9},{9,13},{2,6},{6,10},{10,14},{3,7},{... | collective-permute-start | bytes 589832 | tf_op jit(solution)/shard_map/while/body/eval_jaxpr/ppermute | solution.py:14
  287.0 7.6 %collective-permute-start = (bf16[48,2048]{1,0:T(8,128)(2,1)S(1)}, bf16[48,2048]{1,0:T(8,128)(2,1)S(1)}, u32[]{:S(2)}, u32[]{:S(2)}) collective-permute-start(bf16[48,2048]{1,0:T(8,128)(2,1)S(1)} %get-tuple-element.278), channel_id=1, source_target_pairs={{0,4},{4,8},{8,12},{1,5},{5,9},{9,13},{2,6},{6,10},{10,14},{3,7},{... | collective-permute-start | bytes 589832 | tf_op jit(solution)/shard_map/while/body/eval_jaxpr/ppermute | solution.py:14
  306.4 7.6 %collective-permute-start = (bf16[48,2048]{1,0:T(8,128)(2,1)S(1)}, bf16[48,2048]{1,0:T(8,128)(2,1)S(1)}, u32[]{:S(2)}, u32[]{:S(2)}) collective-permute-start(bf16[48,2048]{1,0:T(8,128)(2,1)S(1)} %get-tuple-element.278), channel_id=1, source_target_pairs={{0,4},{4,8},{8,12},{1,5},{5,9},{9,13},{2,6},{6,10},{10,14},{3,7},{... | collective-permute-start | bytes 589832 | tf_op jit(solution)/shard_map/while/body/eval_jaxpr/ppermute | solution.py:14
  325.8 7.6 %collective-permute-start = (bf16[48,2048]{1,0:T(8,128)(2,1)S(1)}, bf16[48,2048]{1,0:T(8,128)(2,1)S(1)}, u32[]{:S(2)}, u32[]{:S(2)}) collective-permute-start(bf16[48,2048]{1,0:T(8,128)(2,1)S(1)} %get-tuple-element.278), channel_id=1, source_target_pairs={{0,4},{4,8},{8,12},{1,5},{5,9},{9,13},{2,6},{6,10},{10,14},{3,7},{... | collective-permute-start | bytes 589832 | tf_op jit(solution)/shard_map/while/body/eval_jaxpr/ppermute | solution.py:14
  345.2 7.6 %collective-permute-start = (bf16[48,2048]{1,0:T(8,128)(2,1)S(1)}, bf16[48,2048]{1,0:T(8,128)(2,1)S(1)}, u32[]{:S(2)}, u32[]{:S(2)}) collective-permute-start(bf16[48,2048]{1,0:T(8,128)(2,1)S(1)} %get-tuple-element.278), channel_id=1, source_target_pairs={{0,4},{4,8},{8,12},{1,5},{5,9},{9,13},{2,6},{6,10},{10,14},{3,7},{... | collective-permute-start | bytes 589832 | tf_op jit(solution)/shard_map/while/body/eval_jaxpr/ppermute | solution.py:14
  352.7 1.1 copy-start.1
Sparse Core Ops, SparseCore 0:
  9.5 109.1 all-gather.1
where the time goes:
time: 362 us; the launch traced here: 361 us
  waiting for transfers between devices  175 us (48%)
  matrix products  70.3 us (19%)
  local copies, waits for them, and re-layouts  57.7 us (16%)
  other arithmetic  28.4 us (8%)
  starting transfers between devices  14.3 us (4%)
  between operations  14.1 us (4%)
    ppermute x11, waiting for transfers between devices, shifted(): return lax.ppermute(array, axis, pairs)  96.9 us
    all_gather x1, waiting for transfers between devices, per_device(): gathered = lax.all_gather(site_tensor, 'sample', axis=3, tiled=True)[0]  77.5 us
    dot_general x8, matrix products, advance(): jnp.dot(front_rows, masked, preferred_element_type=jnp.float32)  70.3 us
    mul x2, local copies, waits for them, and re-layouts, per_device(): gathered.reshape(blocks, BLOCK, 2, blocks, BLOCK)  32.2 us
    ppermute x11, starting transfers between devices, shifted(): return lax.ppermute(array, axis, pairs)  14.2 us
    unnamed x7, local copies, waits for them, and re-layouts  13.7 us
    select_n x11, other arithmetic, section(): incoming = jnp.where(owner_idx == 0, first_rows, received)  10.7 us
    mul x1, other arithmetic, per_device(): gathered.reshape(blocks, BLOCK, 2, blocks, BLOCK)  9.29 us
  transfers between devices with their start and end apart: 12, of which 12 were waited for; matrix products, arithmetic and copies ran while one was open for 10% of the time, Pallas kernels for 0%

commit v1 on v0

--- a/solution.py
+++ b/solution.py
@@ -30,7 +30,7 @@
     micro_count = 8
     sections = micro_count + site_count - 1
     row_count = fronts_in.shape[0]
-    gathered = lax.all_gather(site_tensor, "sample", axis=3, tiled=True)[0]
+    gathered = jnp.concatenate(lax.all_gather(site_tensor, "sample"), axis=3)[0]
     bond_width = gathered.shape[0]
     blocks = bond_width // BLOCK
     allowed = block_mask(left_charge, right_charge).astype(gathered.dtype)

time: 362 us -> 396 us (1.094)
  waiting for transfers between devices: 175 us -> 202 us
  local copies, waits for them, and re-layouts: 57.7 us -> 65.3 us
    mul x2 -> x1, local copies, waits for them, and re-layouts: 32.2 us -> 2.84 us  [per_device(): gathered.reshape(blocks, BLOCK, 2, blocks, BLOCK)]
    all_gather x1, waiting for transfers between devices: 77.5 us -> 105 us  [per_device(): gathered = jnp.concatenate(lax.all_gather(site_tensor, 'sample'), axis=3)[0]]
    all_gather x0 -> x1, local copies, waits for them, and re-layouts: none -> 21.6 us  [per_device(): gathered = jnp.concatenate(lax.all_gather(site_tensor, 'sample'), axis=3)[0]]
    while x0 -> x1, local copies, waits for them, and re-layouts: none -> 20.8 us  [per_device(): final_state = lax.fori_loop(0, sections, section, initial)]
    unnamed x7 -> x5, local copies, waits for them, and re-layouts: 13.7 us -> 8.27 us
  transfers between devices with their start and end apart: 12 -> 12, of which waited for: 12 -> 12; matrix products, arithmetic and copies ran while one was open for 10% -> 1% of each run, Pallas kernels for 0% -> 0%
where the time goes in v1:
time: 396 us; the launch traced here: 394 us
  waiting for transfers between devices  202 us (51%)
  matrix products  70.3 us (18%)
  local copies, waits for them, and re-layouts  65.3 us (16%)
  other arithmetic  26.5 us (7%)
  starting transfers between devices  14.3 us (4%)
  between operations  14.1 us (4%)
    all_gather x1, waiting for transfers between devices, per_device(): gathered = jnp.concatenate(lax.all_gather(site_tensor, 'sample'), axis=3)[0]  105 us
    ppermute x11, waiting for transfers between devices, shifted(): return lax.ppermute(array, axis, pairs)  96.9 us
    dot_general x8, matrix products, advance(): jnp.dot(front_rows, masked, preferred_element_type=jnp.float32)  70.3 us
    all_gather x1, local copies, waits for them, and re-layouts, per_device(): gathered = jnp.concatenate(lax.all_gather(site_tensor, 'sample'), axis=3)[0]  21.6 us
    while x1, local copies, waits for them, and re-layouts, per_device(): final_state = lax.fori_loop(0, sections, section, initial)  20.8 us
    ppermute x11, starting transfers between devices, shifted(): return lax.ppermute(array, axis, pairs)  14.2 us
    select_n x11, other arithmetic, section(): incoming = jnp.where(owner_idx == 0, first_rows, received)  10.7 us
    unnamed x5, local copies, waits for them, and re-layouts  8.27 us
  transfers between devices with their start and end apart: 12, of which 12 were waited for; matrix products, arithmetic and copies ran while one was open for 1% of the time, Pallas kernels for 0%

profile of v1, /device:TPU:24, one launch (start us, length us, event | category | flops | bytes accessed | tf_op | source)
XLA Modules:
  0.0 393.6 jit_solution(16896623931776280732)
XLA Ops:
  7.2 4.8 %copy.14 = bf16[1,2048,2,512]{3,1,2,0:T(8,128)(2,1)} copy(bf16[1,2048,2,512]{3,2,1,0:T(2,128)(2,1)} %param.8) | data formatting | bytes 8388608 | tf_op args[0]
  13.6 105.5 %all-gather.3.cloned.1.call-done = bf16[4,2048,2,512]{3,1,2,0:T(8,128)(2,1)} async-done(((bf16[1,2048,2,512]{3,1,2,0:T(8,128)(2,1)}), bf16[4,2048,2,512]{3,1,2,0:T(8,128)(2,1)}) %all-gather.3.cloned.1.call-update) | async-done | bytes 16777232 | tf_op jit(solution)/shard_map/all_gather | solution.py:33
  119.1 21.6 %copy.15 = bf16[4,2048,2,512]{1,3,0,2:T(8,128)(2,1)} copy(bf16[4,2048,2,512]{3,1,2,0:T(8,128)(2,1)} %all-gather.3.cloned.1.call-done) | data formatting | bytes 33554432 | tf_op jit(solution)/shard_map/all_gather | solution.py:33
  140.7 2.8 mul.22
  143.5 2.9 copy-done
  146.5 6.8 %bitcast_multiply_fusion = bf16[2048,4096]{0,1:T(8,128)(2,1)} fusion(bf16[512,8,16,128]{3,2,1,0:T(8,128)(2,1)S(1)} %bitcast.35, bf16[4,2048,2,512]{1,3,0,2:T(8,128)(2,1)S(1)} %copy-done), kind=kLoop, calls=%fused_computation.13 | loop fusion | flops 8388608 | bytes 50331648 | tf_op jit(solution)/shard_map/mul | solution.py:38
  153.2 20.8 %copy.16 = bf16[2048,4096]{1,0:T(8,128)(2,1)} copy(bf16[2048,4096]{0,1:T(8,128)(2,1)} %bitcast_multiply_fusion) | data formatting | bytes 33554432 | tf_op jit(solution)/shard_map/while | solution.py:79
  174.3 211.4 %while.18 = (s32[]{:T(128)}, bf16[48,2048]{1,0:T(8,128)(2,1)S(1)}, bf16[384,2048]{1,0:T(8,128)(2,1)S(1)}, f32[384]{0:T(512)S(1)}, s32[]{:T(128)}, /*index=5*/pre...) while((s32[]{:T(128)}, bf16[48,2048]{1,0:T(8,128)(2,1)S(1)}, ...), condition=%wide.region_4.5_spmd, body=%wide.region_0.4_spmd.sunk | while | flops 806092992 | bytes 24644720 | solution.py:79
  174.3 1.0 dynamic-slice_select_fusion.2
  175.3 1.3 collective-permute-start
  176.8 7.4 %collective-permute-done = bf16[48,2048]{1,0:T(8,128)(2,1)S(1)} collective-permute-done((bf16[48,2048]{1,0:T(8,128)(2,1)S(1)}, bf16[48,2048]{1,0:T(8,128)(2,1)S(1)}, u32[]{:S(2)}, u32[]{:S(2)}) %collective-permute-start) | collective-permute-done | bytes 196640 | tf_op jit(solution)/shard_map/while/body/eval_jaxpr/ppermute | solution.py:14
  184.3 1.0 dynamic-slice_select_fusion.2
  185.3 1.3 collective-permute-start
  186.8 6.6 %collective-permute-done = bf16[48,2048]{1,0:T(8,128)(2,1)S(1)} collective-permute-done((bf16[48,2048]{1,0:T(8,128)(2,1)S(1)}, bf16[48,2048]{1,0:T(8,128)(2,1)S(1)}, u32[]{:S(2)}, u32[]{:S(2)}) %collective-permute-start) | collective-permute-done | bytes 196640 | tf_op jit(solution)/shard_map/while/body/eval_jaxpr/ppermute | solution.py:14
  194.4 1.3 collective-permute-start
  195.9 34.7 %collective-permute-done = bf16[48,2048]{1,0:T(8,128)(2,1)S(1)} collective-permute-done((bf16[48,2048]{1,0:T(8,128)(2,1)S(1)}, bf16[48,2048]{1,0:T(8,128)(2,1)S(1)}, u32[]{:S(2)}, u32[]{:S(2)}) %collective-permute-start) | collective-permute-done | bytes 196640 | tf_op jit(solution)/shard_map/while/body/eval_jaxpr/ppermute | solution.py:14
  231.6 10.8 %conditional.2 = (bf16[48,2048]{1,0:T(8,128)(2,1)S(1)}, f32[48]{0:T(128)S(1)}) conditional(s32[]{:T(128)} %convert_element_type.22, bf16[48,2048]{1,0:T(8,128)(2,1)S(1)} %dynamic-slice_select_fusion.2, (s32[384]{0:T(512)S(1)}, s32[]{:T(128)}, bf16[48,2048]{1,0:T(8,128)(2,1)S(1)}, bf16[2048,4096]{1,0:T(8,128)(2,1)}) %tuple.54), branch_computations={%region_1.1_spmd, %region_2.3_spmd} | conditional | flops 805896320 | bytes 22676772 | solution.py:62
  231.6 8.8 %fusion.5 = f32[48,4096]{1,0:T(8,128)S(1)} fusion(bf16[48,2048]{1,0:T(8,128)(2,1)S(1)} %get-tuple-element.177, bf16[2048,4096]{1,0:T(8,128)(2,1)} %get-tuple-element.178), kind=kOutput, calls=%fused_computation.22 | convolution fusion | flops 805306368 | bytes 17760256 | tf_op jit(solution)/shard_map/while/body/eval_jaxpr/cond/branch_1_fun/dot_general | solution.py:44
  242.5 1.3 collective-permute-start
  244.0 6.0 %collective-permute-done = bf16[48,2048]{1,0:T(8,128)(2,1)S(1)} collective-permute-done((bf16[48,2048]{1,0:T(8,128)(2,1)S(1)}, bf16[48,2048]{1,0:T(8,128)(2,1)S(1)}, u32[]{:S(2)}, u32[]{:S(2)}) %collective-permute-start) | collective-permute-done | bytes 196640 | tf_op jit(solution)/shard_map/while/body/eval_jaxpr/ppermute | solution.py:14
  251.0 10.8 %conditional.2 = (bf16[48,2048]{1,0:T(8,128)(2,1)S(1)}, f32[48]{0:T(128)S(1)}) conditional(s32[]{:T(128)} %convert_element_type.22, bf16[48,2048]{1,0:T(8,128)(2,1)S(1)} %dynamic-slice_select_fusion.2, (s32[384]{0:T(512)S(1)}, s32[]{:T(128)}, bf16[48,2048]{1,0:T(8,128)(2,1)S(1)}, bf16[2048,4096]{1,0:T(8,128)(2,1)}) %tuple.54), branch_computations={%region_1.1_spmd, %region_2.3_spmd} | conditional | flops 805896320 | bytes 22676772 | solution.py:62
  251.0 8.8 %fusion.5 = f32[48,4096]{1,0:T(8,128)S(1)} fusion(bf16[48,2048]{1,0:T(8,128)(2,1)S(1)} %get-tuple-element.177, bf16[2048,4096]{1,0:T(8,128)(2,1)} %get-tuple-element.178), kind=kOutput, calls=%fused_computation.22 | convolution fusion | flops 805306368 | bytes 17760256 | tf_op jit(solution)/shard_map/while/body/eval_jaxpr/cond/branch_1_fun/dot_general | solution.py:44
  261.8 1.3 collective-permute-start
  263.4 6.0 %collective-permute-done = bf16[48,2048]{1,0:T(8,128)(2,1)S(1)} collective-permute-done((bf16[48,2048]{1,0:T(8,128)(2,1)S(1)}, bf16[48,2048]{1,0:T(8,128)(2,1)S(1)}, u32[]{:S(2)}, u32[]{:S(2)}) %collective-permute-start) | collective-permute-done | bytes 196640 | tf_op jit(solution)/shard_map/while/body/eval_jaxpr/ppermute | solution.py:14
  270.4 10.8 %conditional.2 = (bf16[48,2048]{1,0:T(8,128)(2,1)S(1)}, f32[48]{0:T(128)S(1)}) conditional(s32[]{:T(128)} %convert_element_type.22, bf16[48,2048]{1,0:T(8,128)(2,1)S(1)} %dynamic-slice_select_fusion.2, (s32[384]{0:T(512)S(1)}, s32[]{:T(128)}, bf16[48,2048]{1,0:T(8,128)(2,1)S(1)}, bf16[2048,4096]{1,0:T(8,128)(2,1)}) %tuple.54), branch_computations={%region_1.1_spmd, %region_2.3_spmd} | conditional | flops 805896320 | bytes 22676772 | solution.py:62
  270.4 8.8 %fusion.5 = f32[48,4096]{1,0:T(8,128)S(1)} fusion(bf16[48,2048]{1,0:T(8,128)(2,1)S(1)} %get-tuple-element.177, bf16[2048,4096]{1,0:T(8,128)(2,1)} %get-tuple-element.178), kind=kOutput, calls=%fused_computation.22 | convolution fusion | flops 805306368 | bytes 17760256 | tf_op jit(solution)/shard_map/while/body/eval_jaxpr/cond/branch_1_fun/dot_general | solution.py:44
  281.2 1.3 collective-permute-start
  282.7 6.0 %collective-permute-done = bf16[48,2048]{1,0:T(8,128)(2,1)S(1)} collective-permute-done((bf16[48,2048]{1,0:T(8,128)(2,1)S(1)}, bf16[48,2048]{1,0:T(8,128)(2,1)S(1)}, u32[]{:S(2)}, u32[]{:S(2)}) %collective-permute-start) | collective-permute-done | bytes 196640 | tf_op jit(solution)/shard_map/while/body/eval_jaxpr/ppermute | solution.py:14
  289.8 10.8 %conditional.2 = (bf16[48,2048]{1,0:T(8,128)(2,1)S(1)}, f32[48]{0:T(128)S(1)}) conditional(s32[]{:T(128)} %convert_element_type.22, bf16[48,2048]{1,0:T(8,128)(2,1)S(1)} %dynamic-slice_select_fusion.2, (s32[384]{0:T(512)S(1)}, s32[]{:T(128)}, bf16[48,2048]{1,0:T(8,128)(2,1)S(1)}, bf16[2048,4096]{1,0:T(8,128)(2,1)}) %tuple.54), branch_computations={%region_1.1_spmd, %region_2.3_spmd} | conditional | flops 805896320 | bytes 22676772 | solution.py:62
  289.8 8.8 %fusion.5 = f32[48,4096]{1,0:T(8,128)S(1)} fusion(bf16[48,2048]{1,0:T(8,128)(2,1)S(1)} %get-tuple-element.177, bf16[2048,4096]{1,0:T(8,128)(2,1)} %get-tuple-element.178), kind=kOutput, calls=%fused_computation.22 | convolution fusion | flops 805306368 | bytes 17760256 | tf_op jit(solution)/shard_map/while/body/eval_jaxpr/cond/branch_1_fun/dot_general | solution.py:44
  300.6 1.3 collective-permute-start
  302.1 6.0 %collective-permute-done = bf16[48,2048]{1,0:T(8,128)(2,1)S(1)} collective-permute-done((bf16[48,2048]{1,0:T(8,128)(2,1)S(1)}, bf16[48,2048]{1,0:T(8,128)(2,1)S(1)}, u32[]{:S(2)}, u32[]{:S(2)}) %collective-permute-start) | collective-permute-done | bytes 196640 | tf_op jit(solution)/shard_map/while/body/eval_jaxpr/ppermute | solution.py:14
  309.1 10.8 %conditional.2 = (bf16[48,2048]{1,0:T(8,128)(2,1)S(1)}, f32[48]{0:T(128)S(1)}) conditional(s32[]{:T(128)} %convert_element_type.22, bf16[48,2048]{1,0:T(8,128)(2,1)S(1)} %dynamic-slice_select_fusion.2, (s32[384]{0:T(512)S(1)}, s32[]{:T(128)}, bf16[48,2048]{1,0:T(8,128)(2,1)S(1)}, bf16[2048,4096]{1,0:T(8,128)(2,1)}) %tuple.54), branch_computations={%region_1.1_spmd, %region_2.3_spmd} | conditional | flops 805896320 | bytes 22676772 | solution.py:62
  309.1 8.8 %fusion.5 = f32[48,4096]{1,0:T(8,128)S(1)} fusion(bf16[48,2048]{1,0:T(8,128)(2,1)S(1)} %get-tuple-element.177, bf16[2048,4096]{1,0:T(8,128)(2,1)} %get-tuple-element.178), kind=kOutput, calls=%fused_computation.22 | convolution fusion | flops 805306368 | bytes 17760256 | tf_op jit(solution)/shard_map/while/body/eval_jaxpr/cond/branch_1_fun/dot_general | solution.py:44
  320.0 1.3 collective-permute-start
  321.5 6.0 %collective-permute-done = bf16[48,2048]{1,0:T(8,128)(2,1)S(1)} collective-permute-done((bf16[48,2048]{1,0:T(8,128)(2,1)S(1)}, bf16[48,2048]{1,0:T(8,128)(2,1)S(1)}, u32[]{:S(2)}, u32[]{:S(2)}) %collective-permute-start) | collective-permute-done | bytes 196640 | tf_op jit(solution)/shard_map/while/body/eval_jaxpr/ppermute | solution.py:14
  328.5 10.8 %conditional.2 = (bf16[48,2048]{1,0:T(8,128)(2,1)S(1)}, f32[48]{0:T(128)S(1)}) conditional(s32[]{:T(128)} %convert_element_type.22, bf16[48,2048]{1,0:T(8,128)(2,1)S(1)} %dynamic-slice_select_fusion.2, (s32[384]{0:T(512)S(1)}, s32[]{:T(128)}, bf16[48,2048]{1,0:T(8,128)(2,1)S(1)}, bf16[2048,4096]{1,0:T(8,128)(2,1)}) %tuple.54), branch_computations={%region_1.1_spmd, %region_2.3_spmd} | conditional | flops 805896320 | bytes 22676772 | solution.py:62
  328.5 8.8 %fusion.5 = f32[48,4096]{1,0:T(8,128)S(1)} fusion(bf16[48,2048]{1,0:T(8,128)(2,1)S(1)} %get-tuple-element.177, bf16[2048,4096]{1,0:T(8,128)(2,1)} %get-tuple-element.178), kind=kOutput, calls=%fused_computation.22 | convolution fusion | flops 805306368 | bytes 17760256 | tf_op jit(solution)/shard_map/while/body/eval_jaxpr/cond/branch_1_fun/dot_general | solution.py:44
  339.3 1.3 collective-permute-start
  340.9 6.0 %collective-permute-done = bf16[48,2048]{1,0:T(8,128)(2,1)S(1)} collective-permute-done((bf16[48,2048]{1,0:T(8,128)(2,1)S(1)}, bf16[48,2048]{1,0:T(8,128)(2,1)S(1)}, u32[]{:S(2)}, u32[]{:S(2)}) %collective-permute-start) | collective-permute-done | bytes 196640 | tf_op jit(solution)/shard_map/while/body/eval_jaxpr/ppermute | solution.py:14
  347.9 10.8 %conditional.2 = (bf16[48,2048]{1,0:T(8,128)(2,1)S(1)}, f32[48]{0:T(128)S(1)}) conditional(s32[]{:T(128)} %convert_element_type.22, bf16[48,2048]{1,0:T(8,128)(2,1)S(1)} %dynamic-slice_select_fusion.2, (s32[384]{0:T(512)S(1)}, s32[]{:T(128)}, bf16[48,2048]{1,0:T(8,128)(2,1)S(1)}, bf16[2048,4096]{1,0:T(8,128)(2,1)}) %tuple.54), branch_computations={%region_1.1_spmd, %region_2.3_spmd} | conditional | flops 805896320 | bytes 22676772 | solution.py:62
  347.9 8.8 %fusion.5 = f32[48,4096]{1,0:T(8,128)S(1)} fusion(bf16[48,2048]{1,0:T(8,128)(2,1)S(1)} %get-tuple-element.177, bf16[2048,4096]{1,0:T(8,128)(2,1)} %get-tuple-element.178), kind=kOutput, calls=%fused_computation.22 | convolution fusion | flops 805306368 | bytes 17760256 | tf_op jit(solution)/shard_map/while/body/eval_jaxpr/cond/branch_1_fun/dot_general | solution.py:44
  358.7 1.3 collective-permute-start
  360.2 6.0 %collective-permute-done = bf16[48,2048]{1,0:T(8,128)(2,1)S(1)} collective-permute-done((bf16[48,2048]{1,0:T(8,128)(2,1)S(1)}, bf16[48,2048]{1,0:T(8,128)(2,1)S(1)}, u32[]{:S(2)}, u32[]{:S(2)}) %collective-permute-start) | collective-permute-done | bytes 196640 | tf_op jit(solution)/shard_map/while/body/eval_jaxpr/ppermute | solution.py:14
  367.2 10.8 %conditional.2 = (bf16[48,2048]{1,0:T(8,128)(2,1)S(1)}, f32[48]{0:T(128)S(1)}) conditional(s32[]{:T(128)} %convert_element_type.22, bf16[48,2048]{1,0:T(8,128)(2,1)S(1)} %dynamic-slice_select_fusion.2, (s32[384]{0:T(512)S(1)}, s32[]{:T(128)}, bf16[48,2048]{1,0:T(8,128)(2,1)S(1)}, bf16[2048,4096]{1,0:T(8,128)(2,1)}) %tuple.54), branch_computations={%region_1.1_spmd, %region_2.3_spmd} | conditional | flops 805896320 | bytes 22676772 | solution.py:62
  367.3 8.8 %fusion.5 = f32[48,4096]{1,0:T(8,128)S(1)} fusion(bf16[48,2048]{1,0:T(8,128)(2,1)S(1)} %get-tuple-element.177, bf16[2048,4096]{1,0:T(8,128)(2,1)} %get-tuple-element.178), kind=kOutput, calls=%fused_computation.22 | convolution fusion | flops 805306368 | bytes 17760256 | tf_op jit(solution)/shard_map/while/body/eval_jaxpr/cond/branch_1_fun/dot_general | solution.py:44
  378.1 1.3 collective-permute-start
  379.6 6.0 %collective-permute-done = bf16[48,2048]{1,0:T(8,128)(2,1)S(1)} collective-permute-done((bf16[48,2048]{1,0:T(8,128)(2,1)S(1)}, bf16[48,2048]{1,0:T(8,128)(2,1)S(1)}, u32[]{:S(2)}, u32[]{:S(2)}) %collective-permute-start) | collective-permute-done | bytes 196640 | tf_op jit(solution)/shard_map/while/body/eval_jaxpr/ppermute | solution.py:14
  (98 shorter events, 30.2 us)
Async XLA Ops:
  7.2 111.9 %all-gather.3.cloned.1.call-start = ((), (), s32[]{:S(2)}) async-start(), calls=%async_computation | async-start | bytes 20971520 | tf_op jit(solution)/shard_map/all_gather | solution.py:33
  140.7 5.8 %copy-start = (bf16[4,2048,2,512]{1,3,0,2:T(8,128)(2,1)S(1)}, bf16[4,2048,2,512]{1,3,0,2:T(8,128)(2,1)}, u32[]{:S(2)}) copy-start(bf16[4,2048,2,512]{1,3,0,2:T(8,128)(2,1)} %copy.15) | copy-start | bytes 50331652
  175.3 9.0 %collective-permute-start = (bf16[48,2048]{1,0:T(8,128)(2,1)S(1)}, bf16[48,2048]{1,0:T(8,128)(2,1)S(1)}, u32[]{:S(2)}, u32[]{:S(2)}) collective-permute-start(bf16[48,2048]{1,0:T(8,128)(2,1)S(1)} %get-tuple-element.287), channel_id=1, source_target_pairs={{0,4},{4,8},{8,12},{1,5},{5,9},{9,13},{2,6},{6,10},{10,14},{3,7},{... | collective-permute-start | bytes 589832 | tf_op jit(solution)/shard_map/while/body/eval_jaxpr/ppermute | solution.py:14
  185.3 8.1 %collective-permute-start = (bf16[48,2048]{1,0:T(8,128)(2,1)S(1)}, bf16[48,2048]{1,0:T(8,128)(2,1)S(1)}, u32[]{:S(2)}, u32[]{:S(2)}) collective-permute-start(bf16[48,2048]{1,0:T(8,128)(2,1)S(1)} %get-tuple-element.287), channel_id=1, source_target_pairs={{0,4},{4,8},{8,12},{1,5},{5,9},{9,13},{2,6},{6,10},{10,14},{3,7},{... | collective-permute-start | bytes 589832 | tf_op jit(solution)/shard_map/while/body/eval_jaxpr/ppermute | solution.py:14
  194.4 36.3 %collective-permute-start = (bf16[48,2048]{1,0:T(8,128)(2,1)S(1)}, bf16[48,2048]{1,0:T(8,128)(2,1)S(1)}, u32[]{:S(2)}, u32[]{:S(2)}) collective-permute-start(bf16[48,2048]{1,0:T(8,128)(2,1)S(1)} %get-tuple-element.287), channel_id=1, source_target_pairs={{0,4},{4,8},{8,12},{1,5},{5,9},{9,13},{2,6},{6,10},{10,14},{3,7},{... | collective-permute-start | bytes 589832 | tf_op jit(solution)/shard_map/while/body/eval_jaxpr/ppermute | solution.py:14
  242.5 7.6 %collective-permute-start = (bf16[48,2048]{1,0:T(8,128)(2,1)S(1)}, bf16[48,2048]{1,0:T(8,128)(2,1)S(1)}, u32[]{:S(2)}, u32[]{:S(2)}) collective-permute-start(bf16[48,2048]{1,0:T(8,128)(2,1)S(1)} %get-tuple-element.287), channel_id=1, source_target_pairs={{0,4},{4,8},{8,12},{1,5},{5,9},{9,13},{2,6},{6,10},{10,14},{3,7},{... | collective-permute-start | bytes 589832 | tf_op jit(solution)/shard_map/while/body/eval_jaxpr/ppermute | solution.py:14
  261.8 7.6 %collective-permute-start = (bf16[48,2048]{1,0:T(8,128)(2,1)S(1)}, bf16[48,2048]{1,0:T(8,128)(2,1)S(1)}, u32[]{:S(2)}, u32[]{:S(2)}) collective-permute-start(bf16[48,2048]{1,0:T(8,128)(2,1)S(1)} %get-tuple-element.287), channel_id=1, source_target_pairs={{0,4},{4,8},{8,12},{1,5},{5,9},{9,13},{2,6},{6,10},{10,14},{3,7},{... | collective-permute-start | bytes 589832 | tf_op jit(solution)/shard_map/while/body/eval_jaxpr/ppermute | solution.py:14
  281.2 7.6 %collective-permute-start = (bf16[48,2048]{1,0:T(8,128)(2,1)S(1)}, bf16[48,2048]{1,0:T(8,128)(2,1)S(1)}, u32[]{:S(2)}, u32[]{:S(2)}) collective-permute-start(bf16[48,2048]{1,0:T(8,128)(2,1)S(1)} %get-tuple-element.287), channel_id=1, source_target_pairs={{0,4},{4,8},{8,12},{1,5},{5,9},{9,13},{2,6},{6,10},{10,14},{3,7},{... | collective-permute-start | bytes 589832 | tf_op jit(solution)/shard_map/while/body/eval_jaxpr/ppermute | solution.py:14
  300.6 7.6 %collective-permute-start = (bf16[48,2048]{1,0:T(8,128)(2,1)S(1)}, bf16[48,2048]{1,0:T(8,128)(2,1)S(1)}, u32[]{:S(2)}, u32[]{:S(2)}) collective-permute-start(bf16[48,2048]{1,0:T(8,128)(2,1)S(1)} %get-tuple-element.287), channel_id=1, source_target_pairs={{0,4},{4,8},{8,12},{1,5},{5,9},{9,13},{2,6},{6,10},{10,14},{3,7},{... | collective-permute-start | bytes 589832 | tf_op jit(solution)/shard_map/while/body/eval_jaxpr/ppermute | solution.py:14
  320.0 7.6 %collective-permute-start = (bf16[48,2048]{1,0:T(8,128)(2,1)S(1)}, bf16[48,2048]{1,0:T(8,128)(2,1)S(1)}, u32[]{:S(2)}, u32[]{:S(2)}) collective-permute-start(bf16[48,2048]{1,0:T(8,128)(2,1)S(1)} %get-tuple-element.287), channel_id=1, source_target_pairs={{0,4},{4,8},{8,12},{1,5},{5,9},{9,13},{2,6},{6,10},{10,14},{3,7},{... | collective-permute-start | bytes 589832 | tf_op jit(solution)/shard_map/while/body/eval_jaxpr/ppermute | solution.py:14
  339.3 7.6 %collective-permute-start = (bf16[48,2048]{1,0:T(8,128)(2,1)S(1)}, bf16[48,2048]{1,0:T(8,128)(2,1)S(1)}, u32[]{:S(2)}, u32[]{:S(2)}) collective-permute-start(bf16[48,2048]{1,0:T(8,128)(2,1)S(1)} %get-tuple-element.287), channel_id=1, source_target_pairs={{0,4},{4,8},{8,12},{1,5},{5,9},{9,13},{2,6},{6,10},{10,14},{3,7},{... | collective-permute-start | bytes 589832 | tf_op jit(solution)/shard_map/while/body/eval_jaxpr/ppermute | solution.py:14
  358.7 7.6 %collective-permute-start = (bf16[48,2048]{1,0:T(8,128)(2,1)S(1)}, bf16[48,2048]{1,0:T(8,128)(2,1)S(1)}, u32[]{:S(2)}, u32[]{:S(2)}) collective-permute-start(bf16[48,2048]{1,0:T(8,128)(2,1)S(1)} %get-tuple-element.287), channel_id=1, source_target_pairs={{0,4},{4,8},{8,12},{1,5},{5,9},{9,13},{2,6},{6,10},{10,14},{3,7},{... | collective-permute-start | bytes 589832 | tf_op jit(solution)/shard_map/while/body/eval_jaxpr/ppermute | solution.py:14
  378.1 7.6 %collective-permute-start = (bf16[48,2048]{1,0:T(8,128)(2,1)S(1)}, bf16[48,2048]{1,0:T(8,128)(2,1)S(1)}, u32[]{:S(2)}, u32[]{:S(2)}) collective-permute-start(bf16[48,2048]{1,0:T(8,128)(2,1)S(1)} %get-tuple-element.287), channel_id=1, source_target_pairs={{0,4},{4,8},{8,12},{1,5},{5,9},{9,13},{2,6},{6,10},{10,14},{3,7},{... | collective-permute-start | bytes 589832 | tf_op jit(solution)/shard_map/while/body/eval_jaxpr/ppermute | solution.py:14
  385.6 1.1 copy-start.1
Sparse Core Ops, SparseCore 0:
  12.2 106.8 all-gather.2
